TPU v7x, 32 devices: a whole 2x2x4 slice. The times are simulated.
32 devices in a mesh: rows: 4 (over y, x), cols: 8 (over z, core).
Axes of the slice: x: 2, y: 2, z: 4, core: 2. Of those that a mesh axis runs over, the one named last changes fastest.
Arguments:
- data_tile: bfloat16 [1024, 8192], P('rows', 'cols'), may hold values from 0.05 to 5
- w_factor: float32 [32, 1024], P(None, ('rows', 'cols')), may hold values from 0.05 to 0.5
- h_factor: float32 [32, 8192], P(None, ('cols', 'rows')), may hold values from 0.05 to 0.5
Outputs:
- w_final: float32 [32, 1024], P(None, ('rows', 'cols'))
- h_final: float32 [32, 8192], P(None, ('cols', 'rows'))
All inputs are finite; a program needn't handle non-finite values.
Results may differ from a plain program's by a relative error of at most 0.00049.
Values may be sent and summed in bfloat16 or wider, within the bound.
A program may use at most 64 MiB of HBM per device.

v0:
```python
import jax
import jax.numpy as jnp
from jax import lax
from jax.sharding import PartitionSpec as P

ITERS = 2


damping = 0.75


def quotient_terms(data_tile, w_block, h_block):
    approx = jnp.einsum("ki,kj->ij", w_block, h_block, preferred_element_type=jnp.float32)
    quotient = (data_tile.astype(jnp.float32) / approx).astype(jnp.bfloat16)
    h_part = jnp.einsum("ki,ij->kj", w_block, quotient, preferred_element_type=jnp.float32)
    w_part = jnp.einsum("kj,ij->ki", h_block, quotient, preferred_element_type=jnp.float32)
    return (h_part, w_part)


def row_sums(block):
    return jnp.sum(block.astype(jnp.float32), axis=1)


def totals(w_own, h_own):
    w_total, h_total = lax.psum((row_sums(w_own), row_sums(h_own)), ("rows", "cols"))
    return (w_total, h_total)


def scaled(factor, numer, total):
    return factor * (1.0 - damping + damping * numer / total[:, None])


def shards(data_tile, w_factor, h_factor):
    w_now = w_factor
    h_now = h_factor
    for rounds in range(ITERS):
        w_round = w_now.astype(jnp.bfloat16)
        h_round = h_now.astype(jnp.bfloat16)
        w_block = lax.all_gather(w_round, "cols", axis=1, tiled=True)
        h_block = lax.all_gather(h_round, "rows", axis=1, tiled=True)
        h_part, w_part = quotient_terms(data_tile, w_block, h_block)
        h_numer = lax.psum_scatter(h_part, "rows", scatter_dimension=1, tiled=True)
        w_numer = lax.psum_scatter(w_part, "cols", scatter_dimension=1, tiled=True)
        w_total, h_total = totals(w_round, h_round)
        h_next = scaled(h_now, h_numer, w_total)
        w_next = scaled(w_now, w_numer, h_total)
        w_now = w_next
        h_now = h_next
    return (w_now, h_now)


def solution(mesh):
    placed = (P("rows", "cols"), P(None, ("rows", "cols")), P(None, ("cols", "rows")))
    return jax.shard_map(
        shards,
        mesh=mesh,
        in_specs=placed,
        out_specs=(P(None, ("rows", "cols")), P(None, ("cols", "rows"))),
        check_vma=False,
    )
```

profile of v0, /device:TPU:0, one launch (start us, length us, event | category | flops | bytes accessed | tf_op | source)
XLA Modules:
  0.0 165.2 jit_solution(12160451287689017585)
XLA Ops:
  7.2 0.0 reduce-scatter.13.cloned.1.call-start
  7.2 0.9 convert_reduce_fusion.1
  8.1 0.0 copy-start.1
  8.1 10.1 %all_gather.13 = bf16[32,1024]{1,0:T(8,128)(2,1)S(1)} all-gather(bf16[32,256]{1,0:T(8,128)(2,1)S(1)} %get-tuple-element.11), channel_id=1, replica_groups=mesh['rows'=4,'cols'=8] {'rows'}, dimensions={1}, use_global_device_ids=true | all-gather | bytes 81920 | tf_op jit(solution)/shard_map/all_gather | solution.py:40
  18.2 0.0 copy-done.1
  18.2 0.1 copy.5
  18.2 14.2 %all_gather.12 = bf16[32,256]{0,1:T(8,128)(2,1)S(1)} all-gather(bf16[32,32]{0,1:T(8,128)(2,1)S(1)} %copy.5), channel_id=1, replica_groups=mesh['rows'=4,'cols'=8] {'cols'}, dimensions={1}, use_global_device_ids=true | all-gather | bytes 18432 | tf_op jit(solution)/shard_map/all_gather | solution.py:39
  32.4 1.3 fusion
  33.8 0.2 convolution_bitcast_fusion.2
  34.0 0.8 copy.7
  34.8 0.0 reduce-scatter.13.cloned.1.call-update
  34.8 0.0 copy-start.3
  34.8 0.0 reduce-scatter.9.cloned.1.call-start
  34.9 0.9 convolution_bitcast_fusion.1
  35.8 0.0 reduce-scatter.9.cloned.1.call-update
  35.8 0.0 reduce-scatter.15.cloned.1.call-start
  35.9 39.3 %all-reduce.1 = (f32[32]{0:T(128)S(1)}, f32[32]{0:T(128)S(1)}) all-reduce(f32[32]{0:T(128)S(1)} %convert_reduce_fusion.3, f32[32]{0:T(128)S(1)} %get-tuple-element.10), channel_id=1, replica_groups=mesh['rows'=4,'cols'=8] {'rows','cols'}, use_global_device_ids=true, to_apply=%region_5.0 | all-reduce | flops 64 | bytes 512 | tf_op jit(solution)/shard_map/psum | solution.py:25
  75.2 0.0 reduce-scatter.13.cloned.1.call-done
  75.2 0.8 copy.8
  76.0 0.2 convert_reduce_fusion.2
  76.2 0.1 copy.6
  76.2 0.0 copy-start
  76.2 14.1 %all_gather.15 = bf16[32,256]{0,1:T(8,128)(2,1)S(1)} all-gather(bf16[32,32]{0,1:T(8,128)(2,1)S(1)} %copy.6), channel_id=1, replica_groups=mesh['rows'=4,'cols'=8] {'cols'}, dimensions={1}, use_global_device_ids=true | all-gather | bytes 18432 | tf_op jit(solution)/shard_map/all_gather | solution.py:39
  90.4 0.4 reduce-scatter.9.cloned.1.call-done
  90.8 0.0 copy-done
  90.8 0.9 convert_reduce_fusion
  91.7 8.8 %all_gather.14 = bf16[32,1024]{1,0:T(8,128)(2,1)S(1)} all-gather(bf16[32,256]{1,0:T(8,128)(2,1)S(1)} %get-tuple-element.9), channel_id=1, replica_groups=mesh['rows'=4,'cols'=8] {'rows'}, dimensions={1}, use_global_device_ids=true | all-gather | bytes 81920 | tf_op jit(solution)/shard_map/all_gather | solution.py:40
  100.5 0.0 copy-done.3
  100.5 0.3 fusion.1
  100.8 0.9 convolution_bitcast_fusion
  101.7 0.0 reduce-scatter.15.cloned.1.call-update
  101.7 0.0 reduce-scatter.11.cloned.1.call-start
  101.8 0.9 fusion.6
  102.7 0.0 reduce-scatter.11.cloned.1.call-update
  102.7 39.0 %all-reduce = (f32[32]{0:T(128)S(1)}, f32[32]{0:T(128)S(1)}) all-reduce(f32[32]{0:T(128)S(1)} %get-tuple-element.8, f32[32]{0:T(128)S(1)} %get-tuple-element.6), channel_id=1, replica_groups=mesh['rows'=4,'cols'=8] {'rows','cols'}, use_global_device_ids=true, to_apply=%region_8.0 | all-reduce | flops 64 | bytes 512 | tf_op jit(solution)/shard_map/psum | solution.py:25
  141.7 0.0 reduce-scatter.15.cloned.1.call-done
  141.7 0.8 copy.10
  142.5 0.0 copy-start.2
  142.5 0.7 add_multiply_fusion.2
  143.2 14.1 %reduce-scatter.11.cloned.1.call-done = f32[32,256]{1,0:T(8,128)} async-done(((f32[32,1024]{1,0:T(8,128)}), f32[32,256]{1,0:T(8,128)}) %reduce-scatter.11.cloned.1.call-update) | async-done | bytes 32784 | tf_op jit(solution)/shard_map/reduce_scatter | solution.py:42
  157.2 0.0 copy-done.2
  157.2 1.5 add_multiply_fusion
  (1 shorter events, 0.0 us)
Async XLA Ops:
  7.2 68.0 %reduce-scatter.13.cloned.1.call-start = ((), (), s32[]{:S(2)}) async-start(), calls=%async_computation.6 | async-start | bytes 147456
  8.1 10.1 %copy-start.1 = (f32[32,32]{1,0:T(8,128)S(1)}, f32[32,32]{1,0:T(8,128)}, u32[]{:S(2)}) copy-start(f32[32,32]{1,0:T(8,128)} %param.4) | copy-start | bytes 12292
  34.8 65.7 %copy-start.3 = (bf16[256,1024]{1,0:T(8,128)(2,1)S(1)}, bf16[256,1024]{1,0:T(8,128)(2,1)}, u32[]{:S(2)}) copy-start(bf16[256,1024]{1,0:T(8,128)(2,1)} %param.3) | copy-start | bytes 1572868
  34.8 55.9 %reduce-scatter.9.cloned.1.call-start = ((), (), s32[]{:S(2)}) async-start(), calls=%async_computation.4 | async-start | bytes 163840 | tf_op jit(solution)/shard_map/reduce_scatter | solution.py:42
  35.8 105.9 %reduce-scatter.15.cloned.1.call-start = ((), (), s32[]{:S(2)}) async-start(), calls=%async_computation.7 | async-start | bytes 147456
  76.2 14.5 %copy-start = (f32[32,256]{1,0:T(8,128)S(1)}, f32[32,256]{1,0:T(8,128)}, u32[]{:S(2)}) copy-start(f32[32,256]{1,0:T(8,128)} %param.5) | copy-start | bytes 98308
  101.7 55.5 %reduce-scatter.11.cloned.1.call-start = ((), (), s32[]{:S(2)}) async-start(), calls=%async_computation.5 | async-start | bytes 163840 | tf_op jit(solution)/shard_map/reduce_scatter | solution.py:42
  142.5 14.8 %copy-start.2 = (f32[32,256]{1,0:T(8,128)S(1)}, f32[32,256]{1,0:T(8,128)}, u32[]{:S(2)}) copy-start(f32[32,256]{1,0:T(8,128)} %reduce-scatter.9.cloned.1.call-done) | copy-start | bytes 98308
Sparse Core Ops, SparseCore 0:
  34.9 30.7 reduce-scatter.12
  68.4 22.2 reduce-scatter.8
  101.9 30.2 reduce-scatter.14
  134.7 22.4 reduce-scatter.10
where the time goes:
time: 166 us; the launch traced here: 165 us
  blocking collectives  126 us (76%)
  waiting for transfers between devices  14.5 us (9%)
  between operations  13.8 us (8%)
  matrix products  4.5 us (3%)
  other arithmetic  4.17 us (3%)
  local copies, waits for them, and re-layouts  2.53 us (2%)
    psum x2, blocking collectives, totals(): lax.psum((row_sums(w_own), row_sums(h_own)), ('rows', 'cols'))  78.3 us
    all_gather x2, blocking collectives, shards(): w_block = lax.all_gather(w_round, 'cols', axis=1, tiled=True)  28.3 us
    all_gather x2, blocking collectives, shards(): h_block = lax.all_gather(h_round, 'rows', axis=1, tiled=True)  18.9 us
    reduce_scatter x2, waiting for transfers between devices, shards(): h_numer = lax.psum_scatter(h_part, 'rows', scatter_dimension=1, tiled=True)  14.5 us
  transfers between devices with their start and end apart: 4, of which 2 were waited for; matrix products, arithmetic and copies ran while one was open for 3% of the time, Pallas kernels for 0%

commit v1 on v0

v1 whole, which is shorter than its diff:
```python
import functools

import jax
import jax.numpy as jnp
from jax import lax
from jax.experimental import pallas as pl
from jax.experimental.pallas import tpu as pltpu
from jax.sharding import PartitionSpec as P

ITERS = 2

damping = 0.75

MESH = pl.DeviceIdType.MESH
SUB = 8
LANES = 128


def partner(me, d, n):
    if n & (n - 1) == 0:
        out, bit = me, 1
        while bit < n:
            if d & bit:
                out = out + bit * (1 - 2 * (lax.rem(lax.div(me, bit), 2)))
            bit *= 2
        return out
    return lax.rem(d + n - me, n)


def fold(block):
    return jnp.concatenate([block[s : s + SUB] for s in range(0, block.shape[0], SUB)], axis=1)


def unfold(dense, groups, width):
    return jnp.concatenate([dense[:, s * width : (s + 1) * width] for s in range(groups)], axis=0)


def kernel(
    rows, cols, data_hbm, w_hbm, h_hbm, w_out, h_out,
    data_v, w_in, h_own, w_own, w_slots, h_slots, h_send, h_recv, w_send, w_recv,
    local_sem, wg_s, wg_r, hg_s, hg_r, hr_s, hr_r, wr_s, wr_r,
):
    c, r = lax.axis_index("cols"), lax.axis_index("rows")
    rank, wp = w_hbm.shape
    hp = h_hbm.shape[1]
    tr, tc = data_v.shape
    groups = rank // SUB
    used = groups * wp

    load_w = pltpu.make_async_copy(w_hbm, w_in, local_sem.at[0])
    load_h = pltpu.make_async_copy(h_hbm, h_own, local_sem.at[1])
    load_data = pltpu.make_async_copy(data_hbm, data_v, local_sem.at[2])
    load_w.start()
    load_h.start()
    load_data.start()

    c_peers = [(d, partner(c, d, cols)) for d in range(1, cols)]
    r_peers = [(d, partner(r, d, rows)) for d in range(1, rows)]
    barrier = pltpu.get_barrier_semaphore()
    for d, p in c_peers:
        pl.semaphore_signal(barrier, inc=1, device_id={"cols": p}, device_id_type=MESH)
    for d, p in r_peers:
        pl.semaphore_signal(barrier, inc=1, device_id={"rows": p}, device_id_type=MESH)

    load_w.wait()
    load_h.wait()

    def put_w(it, dense):
        w_own[it, :, 0:used] = dense

    put_w(0, fold(w_in[...]))
    h_slots[0, 0] = h_own[...].astype(jnp.bfloat16)
    pl.semaphore_wait(barrier, cols - 1 + rows - 1)

    pending = []

    def send(src, dst, s_sem, r_sem, where):
        copy = pltpu.make_async_remote_copy(
            src_ref=src, dst_ref=dst, send_sem=s_sem, recv_sem=r_sem, device_id=where, device_id_type=MESH
        )
        copy.start()
        pending.append(copy)
        return copy

    def gather_w(it):
        return [
            send(w_own.at[it], w_slots.at[it, c], wg_s.at[it, d], wg_r.at[it, d], {"cols": p})
            for d, p in reversed(c_peers)
        ]

    def gather_h(it):
        return {
            d: send(h_slots.at[it, 0], h_slots.at[it, d], hg_s.at[it, d], hg_r.at[it, d], {"rows": p})
            for d, p in reversed(r_peers)
        }

    w_copies = gather_w(0)
    h_copies = gather_h(0)
    w_dense = w_own[0, :, 0:used]
    h_now = h_own[...]

    for it in range(ITERS):
        w_slots[it, c] = w_own[it]
        for copy in w_copies:
            copy.wait_recv()
        w_f32 = jnp.concatenate(
            [
                jnp.concatenate([w_slots[it, p, :, s * wp : (s + 1) * wp] for p in range(cols)], axis=1)
                for s in range(groups)
            ],
            axis=0,
        )
        w_block = w_f32.astype(jnp.bfloat16)
        w_rows = w_f32.T.astype(jnp.bfloat16)
        w_sum = jnp.sum(w_block.astype(jnp.float32), axis=1, keepdims=True)
        w_sum = fold(jnp.broadcast_to(w_sum, (rank, hp // groups)))
        if it == 0:
            load_data.wait()
        w_part = jnp.zeros((rank, tr), jnp.float32)
        h_sum = jnp.zeros((rank, 1), jnp.float32)
        h_sends = []
        for d in range(rows):
            p = r if d == 0 else r_peers[d - 1][1]
            if d > 0:
                h_copies[d].wait_recv()
            h_piece = h_slots[it, d]
            approx = jnp.dot(w_rows, h_piece, preferred_element_type=jnp.float32)
            if hp % LANES == 0:
                data = data_v[:, pl.ds(pl.multiple_of(p * hp, hp), hp)]
            else:
                per = LANES // hp
                base = pl.multiple_of(lax.div(p, per) * LANES, LANES)
                wide = data_v[:, pl.ds(base, LANES)].astype(jnp.float32)
                data = wide[:, 0:hp]
                for k in range(1, per):
                    data = jnp.where(lax.rem(p, per) == k, wide[:, k * hp : (k + 1) * hp], data)
            quotient = (data.astype(jnp.float32) / approx).astype(jnp.bfloat16)
            h_part = jnp.dot(w_block, quotient, preferred_element_type=jnp.float32)
            h_send[it, d, 0:rank] = h_part
            h_send[it, d, rank : rank + SUB] = w_sum
            if d > 0:
                h_sends.append(
                    send(h_send.at[it, d], h_recv.at[it, d], hr_s.at[it, d], hr_r.at[it, d], {"rows": p})
                )
            w_part += lax.dot_general(
                h_piece, quotient, (((1,), (1,)), ((), ())), preferred_element_type=jnp.float32
            )
            h_sum += jnp.sum(h_piece.astype(jnp.float32), axis=1, keepdims=True)

        h_sum = fold(jnp.broadcast_to(h_sum, (rank, wp)))
        for p in range(cols):
            w_send[it, p, 0, :, 0:used] = fold(w_part[:, p * wp : (p + 1) * wp])
            w_send[it, p, 1, :, 0:used] = h_sum
        w_sends = [
            send(w_send.at[it, p], w_recv.at[it, d], wr_s.at[it, d], wr_r.at[it, d], {"cols": p})
            for d, p in reversed(c_peers)
        ]

        total = h_send[it, 0]
        for copy in h_sends:
            copy.wait_recv()
        for d, p in r_peers:
            total += h_recv[it, d]
        w_total = unfold(total[rank : rank + SUB], groups, hp // groups)[:, 0:1]
        h_now = h_now * (1.0 - damping + damping * total[0:rank] / w_total)
        if it + 1 < ITERS:
            h_slots[it + 1, 0] = h_now.astype(jnp.bfloat16)
            h_copies = gather_h(it + 1)
        else:
            h_out[...] = h_now

        total = w_send[it, c]
        for copy in w_sends:
            copy.wait_recv()
        for d, p in c_peers:
            total += w_recv[it, d]
        numer, h_total = total[0, :, 0:used], total[1, :, 0:used]
        w_dense = w_dense * (1.0 - damping + damping * numer / h_total)
        if it + 1 < ITERS:
            put_w(it + 1, w_dense)
            w_copies = gather_w(it + 1)
        else:
            w_out[...] = unfold(w_dense, groups, wp)

    for copy in pending:
        copy.wait_send()


def solution(mesh):
    rows, cols = mesh.shape["rows"], mesh.shape["cols"]

    def shards(data_tile, w_factor, h_factor):
        rank, wp = w_factor.shape
        hp = h_factor.shape[1]
        wide = pl.cdiv(rank // SUB * wp, LANES) * LANES
        vmem, dma = pltpu.VMEM, pltpu.SemaphoreType.DMA
        return pl.pallas_call(
            functools.partial(kernel, rows, cols),
            out_shape=(
                jax.ShapeDtypeStruct(w_factor.shape, jnp.float32),
                jax.ShapeDtypeStruct(h_factor.shape, jnp.float32),
            ),
            in_specs=[pl.BlockSpec(memory_space=pl.ANY)] * 3,
            out_specs=(pl.BlockSpec(memory_space=pltpu.VMEM),) * 2,
            scratch_shapes=[
                vmem(data_tile.shape, jnp.bfloat16),
                vmem(w_factor.shape, jnp.float32),
                vmem(h_factor.shape, jnp.float32),
                vmem((ITERS, SUB, wide), jnp.float32),
                vmem((ITERS, cols, SUB, wide), jnp.float32),
                vmem((ITERS, rows, rank, hp), jnp.bfloat16),
                vmem((ITERS, rows, rank + SUB, hp), jnp.float32),
                vmem((ITERS, rows, rank + SUB, hp), jnp.float32),
                vmem((ITERS, cols, 2, SUB, wide), jnp.float32),
                vmem((ITERS, cols, 2, SUB, wide), jnp.float32),
                dma((3,)),
                dma((ITERS, cols)),
                dma((ITERS, cols)),
                dma((ITERS, rows)),
                dma((ITERS, rows)),
                dma((ITERS, rows)),
                dma((ITERS, rows)),
                dma((ITERS, cols)),
                dma((ITERS, cols)),
            ],
            compiler_params=pltpu.CompilerParams(collective_id=0, has_side_effects=True),
        )(data_tile, w_factor, h_factor)

    placed = (P("rows", "cols"), P(None, ("rows", "cols")), P(None, ("cols", "rows")))
    return jax.shard_map(
        shards,
        mesh=mesh,
        in_specs=placed,
        out_specs=(P(None, ("rows", "cols")), P(None, ("cols", "rows"))),
        check_vma=False,
    )
```

time: 166 us -> 27.3 us (0.16)
  blocking collectives: 126 us -> 0 us
  Pallas kernels: 0 us -> 24.4 us
  waiting for transfers between devices: 14.5 us -> 0 us
  between operations: 13.8 us -> 0.65 us
  matrix products: 4.5 us -> 0 us
  other arithmetic: 4.17 us -> 0 us
    psum x2 -> x0, blocking collectives: 78.3 us -> none  [totals(): lax.psum((row_sums(w_own), row_sums(h_own)), ('rows', 'cols'))]
    all_gather x4 -> x0, blocking collectives: 47.2 us -> none  [the longest x2 28.3 us: shards(): w_block = lax.all_gather(w_round, 'cols', axis=1, tiled=True)]
    pallas_call x0 -> x1, Pallas kernels: none -> 24.4 us  [shards(): pl.pallas_call(functools.partial(kernel, rows, cols), out_shape=(jax.Shap...]
    reduce_scatter x2 -> x0, waiting for transfers between devices: 14.5 us -> none  [shards(): h_numer = lax.psum_scatter(h_part, 'rows', scatter_dimension=1, tiled=True)]
    dot_general x5 -> x0, matrix products: 3.58 us -> none  [the longest x2 1.75 us: quotient_terms(): jnp.einsum('ki,ij->kj', w_block, quotient, preferred_element_type=jnp.flo...]
    mul x2 -> x0, other arithmetic: 2.15 us -> none  [scaled(): return factor * (1.0 - damping + damping * numer / total[:, None])]
    reduce_sum x4 -> x0, other arithmetic: 2.02 us -> none  [row_sums(): return jnp.sum(block.astype(jnp.float32), axis=1)]
  transfers between devices with their start and end apart: 4 -> 0, of which waited for: 2 -> 0; matrix products, arithmetic and copies ran while one was open for 3% -> 0% of each run, Pallas kernels for 0% -> 0%
where the time goes in v1:
time: 27.3 us; the launch traced here: 27 us
  Pallas kernels  24.4 us (89%)
  local copies, waits for them, and re-layouts  1.95 us (7%)
  between operations  0.65 us (2%)
    pallas_call x1, Pallas kernels, shards(): pl.pallas_call(functools.partial(kernel, rows, cols), out_shape=(jax.Shap...  24.4 us
    unnamed x4, local copies, waits for them, and re-layouts  1.95 us

profile of v1, /device:TPU:0, one launch (start us, length us, event | category | flops | bytes accessed | tf_op | source)
XLA Modules:
  0.0 27.0 jit_solution(11665787069295942553)
XLA Ops:
  0.6 24.4 %shard_map.50 = (f32[32,32]{1,0:T(8,128)}, f32[32,256]{1,0:T(8,128)}) custom-call(bf16[256,1024]{1,0:T(8,128)(2,1)} %data_hbm.1, f32[32,32]{1,0:T(8,128)} %w_hbm.1, f32[32,256]{1,0:T(8,128)} %h_hbm.1), custom_call_target="tpu_custom_call" | custom-call | tf_op jit(solution)/shard_map/pallas_call | solution.py:197
  25.1 0.0 copy-start
  25.1 1.3 %copy.7 = f32[32,32]{1,0:T(8,128)} copy(f32[32,32]{1,0:T(8,128)} %get-tuple-element.4) | data formatting | bytes 8192
  26.4 0.0 copy-done
  26.4 0.6 %copy.8 = f32[32,256]{1,0:T(8,128)} copy(f32[32,256]{1,0:T(8,128)S(1)} %copy-done) | data formatting | bytes 65536
Async XLA Ops:
  25.1 1.3 %copy-start = (f32[32,256]{1,0:T(8,128)S(1)}, f32[32,256]{1,0:T(8,128)}, u32[]{:S(2)}) copy-start(f32[32,256]{1,0:T(8,128)} %get-tuple-element.5) | copy-start | bytes 98308

commit v2 on v1

v2 whole, which is shorter than its diff:
```python
import functools

import jax
import jax.numpy as jnp
from jax import lax
from jax.experimental import pallas as pl
from jax.experimental.pallas import tpu as pltpu
from jax.sharding import PartitionSpec as P

ITERS = 2

damping = 0.75

MESH = pl.DeviceIdType.MESH
SUB = 8
LANES = 128


def partner(me, d, n):
    if n & (n - 1) == 0:
        out, bit = me, 1
        while bit < n:
            if d & bit:
                out = out + bit * (1 - 2 * (lax.rem(lax.div(me, bit), 2)))
            bit *= 2
        return out
    return lax.rem(d + n - me, n)


def fold(block):
    return jnp.concatenate([block[s : s + SUB] for s in range(0, block.shape[0], SUB)], axis=1)


def unfold(dense, groups, width):
    return jnp.concatenate([dense[:, s * width : (s + 1) * width] for s in range(groups)], axis=0)


def chunk_order(it, rows):
    return [*range(rows - 1, 0, -1), 0]


def as_column(row, rank):
    spread = jnp.broadcast_to(row[:, 0:rank], (rank, rank))
    at = lax.broadcasted_iota(jnp.int32, (rank, rank), 0) == lax.broadcasted_iota(jnp.int32, (rank, rank), 1)
    return jnp.sum(jnp.where(at, spread, 0.0), axis=1, keepdims=True)


def kernel(
    rows, cols, data_hbm, w_hbm, h_hbm, w_out, h_out,
    data_v, w_in, h_own, w_own, w_slots, h_slots, h_send, h_recv, w_send, w_recv,
    pair_send, pair_recv, chip_sums, half_send, half_recv,
    local_sem, wg_s, wg_r, hg_s, hg_r, hr_s, hr_r, wr_s, wr_r, ps_s, ps_r, cs_s, cs_r, hf_s, hf_r,
):
    c, r = lax.axis_index("cols"), lax.axis_index("rows")
    rank, wp = w_hbm.shape
    hp = h_hbm.shape[1]
    tr, tc = data_v.shape
    groups = rank // SUB
    used = groups * wp
    half = tr // 2
    chips = cols // 2
    chip, core = lax.div(c, 2), lax.rem(c, 2)

    load_w = pltpu.make_async_copy(w_hbm, w_in, local_sem.at[0])
    load_h = pltpu.make_async_copy(h_hbm, h_own, local_sem.at[1])
    load_data = pltpu.make_async_copy(data_hbm, data_v, local_sem.at[2])
    load_w.start()
    load_h.start()
    load_data.start()

    c_peers = [(d, partner(c, d, cols)) for d in range(1, cols)]
    r_peers = [(d, partner(r, d, rows)) for d in range(1, rows)]
    chip_peers = [(d, 2 * partner(chip, d, chips) + core) for d in range(1, chips)]
    barrier = pltpu.get_barrier_semaphore()
    for d, p in reversed(c_peers):
        pl.semaphore_signal(barrier, inc=1, device_id={"cols": p}, device_id_type=MESH)
    for d, p in reversed(r_peers):
        pl.semaphore_signal(barrier, inc=1, device_id={"rows": p}, device_id_type=MESH)

    load_w.wait()
    load_h.wait()
    w_own[:, 0:used] = fold(w_in[...])
    h_slots[0, 0] = h_own[...].astype(jnp.bfloat16)
    pl.semaphore_wait(barrier, cols - 1 + rows - 1)

    pending = []

    def send(src, dst, s_sem, r_sem, where):
        copy = pltpu.make_async_remote_copy(
            src_ref=src, dst_ref=dst, send_sem=s_sem, recv_sem=r_sem, device_id=where, device_id_type=MESH
        )
        copy.start()
        pending.append(copy)
        return copy

    def gather_h(it):
        return {
            d: send(h_slots.at[it, 0], h_slots.at[it, d], hg_s.at[it, d], hg_r.at[it, d], {"rows": p})
            for d, p in reversed(r_peers)
        }

    w_copies = [
        send(w_own, w_slots.at[c], wg_s.at[d], wg_r.at[d], {"cols": p}) for d, p in reversed(c_peers)
    ]
    h_copies = gather_h(0)
    h_now = h_own[...]
    w_slots[c] = w_own[...]
    load_data.wait()
    for copy in w_copies:
        copy.wait_recv()
    w_f32 = jnp.concatenate(
        [
            jnp.concatenate([w_slots[p, :, s * wp : (s + 1) * wp] for p in range(cols)], axis=1)
            for s in range(groups)
        ],
        axis=0,
    )

    for it in range(ITERS):
        last = it + 1 == ITERS
        w_block = w_f32.astype(jnp.bfloat16)
        w_rows = w_f32.T.astype(jnp.bfloat16)
        w_sum = jnp.sum(w_rows.astype(jnp.float32), axis=0, keepdims=True)
        w_part = jnp.zeros((rank, tr), jnp.float32)
        h_sum = jnp.zeros((SUB, rank), jnp.float32)
        h_sends = []
        for d in chunk_order(it, rows):
            p = r if d == 0 else r_peers[d - 1][1]
            if d > 0:
                h_copies[d].wait_recv()
            h_piece = h_slots[it, d]
            approx = jnp.dot(w_rows, h_piece, preferred_element_type=jnp.float32)
            if hp % LANES == 0:
                data = data_v[:, pl.ds(pl.multiple_of(p * hp, hp), hp)]
            else:
                per = LANES // hp
                base = pl.multiple_of(lax.div(p, per) * LANES, LANES)
                wide = data_v[:, pl.ds(base, LANES)].astype(jnp.float32)
                data = wide[:, 0:hp]
                for k in range(1, per):
                    data = jnp.where(lax.rem(p, per) == k, wide[:, k * hp : (k + 1) * hp], data)
            quotient = (data.astype(jnp.float32) / approx).astype(jnp.bfloat16)
            h_part = jnp.dot(w_block, quotient, preferred_element_type=jnp.float32)
            h_send[it, d, 0:rank] = h_part
            h_send[it, d, rank : rank + 1, 0:rank] = w_sum
            if d > 0:
                h_sends.append(
                    send(h_send.at[it, d], h_recv.at[it, d], hr_s.at[it, d], hr_r.at[it, d], {"rows": p})
                )
            w_part += lax.dot_general(
                h_piece, quotient, (((1,), (1,)), ((), ())), preferred_element_type=jnp.float32
            )
            h_sum += lax.dot_general(
                jnp.ones((SUB, hp), jnp.bfloat16), h_piece, (((1,), (1,)), ((), ())),
                preferred_element_type=jnp.float32,
            )

        if last:
            for p in range(cols):
                w_send[p, 0:SUB, 0:used] = fold(w_part[:, p * wp : (p + 1) * wp])
                w_send[p, SUB : SUB + 1, 0:rank] = h_sum[0:1]
            w_sends = [
                send(w_send.at[p], w_recv.at[d], wr_s.at[d], wr_r.at[d], {"cols": p})
                for d, p in reversed(c_peers)
            ]
        else:
            low, high = w_part[:, 0:half], w_part[:, half:tr]
            pair_send[it, 0:rank] = jnp.where(core == 0, high, low)
            pair_send[it, rank : rank + 1, 0:rank] = h_sum[0:1]
            pair = send(
                pair_send.at[it], pair_recv.at[it], ps_s.at[it], ps_r.at[it], {"cols": c + 1 - 2 * core}
            )
            kept = jnp.where(core == 0, low, high)
            pair.wait_recv()
            chip_sums[it, chip, 0:rank] = kept + pair_recv[it, 0:rank]
            chip_sums[it, chip, rank : rank + 1, 0:rank] = h_sum[0:1] + pair_recv[it, rank : rank + 1, 0:rank]
            chip_sends = [
                send(
                    chip_sums.at[it, chip], chip_sums.at[it, chip], cs_s.at[it, d], cs_r.at[it, d], {"cols": p}
                )
                for d, p in reversed(chip_peers)
            ]

        for copy in h_sends:
            copy.wait_recv()
        numer, total = h_send[it, 0, 0:rank], h_send[it, 0, rank : rank + 1, 0:rank]
        for d, p in r_peers:
            numer += h_recv[it, d, 0:rank]
            total += h_recv[it, d, rank : rank + 1, 0:rank]
        h_now = h_now * (1.0 - damping + damping * numer / as_column(total, rank))
        if last:
            h_out[...] = h_now
        else:
            h_slots[it + 1, 0] = h_now.astype(jnp.bfloat16)
            h_copies = gather_h(it + 1)

        if last:
            w_now = w_f32[:, 0:wp]
            for p in range(1, cols):
                w_now = jnp.where(c == p, w_f32[:, p * wp : (p + 1) * wp], w_now)
            for copy in w_sends:
                copy.wait_recv()
            numer, total = w_send[c, 0:SUB, 0:used], w_send[c, SUB : SUB + 1, 0:rank]
            for d, p in c_peers:
                numer += w_recv[d, 0:SUB, 0:used]
                total += w_recv[d, SUB : SUB + 1, 0:rank]
            numer = unfold(numer, groups, wp)
            w_out[...] = w_now * (1.0 - damping + damping * numer / as_column(total, rank))
        else:
            w_half = jnp.where(core == 0, w_f32[:, 0:half], w_f32[:, half:tr])
            for copy in chip_sends:
                copy.wait_recv()
            numer, total = chip_sums[it, 0, 0:rank], chip_sums[it, 0, rank : rank + 1, 0:rank]
            for p in range(1, chips):
                numer += chip_sums[it, p, 0:rank]
                total += chip_sums[it, p, rank : rank + 1, 0:rank]
            w_half = w_half * (1.0 - damping + damping * numer / as_column(total, rank))
            half_send[it] = w_half
            swap = send(
                half_send.at[it], half_recv.at[it], hf_s.at[it], hf_r.at[it], {"cols": c + 1 - 2 * core}
            )
            swap.wait_recv()
            theirs = half_recv[it]
            w_f32 = jnp.concatenate(
                [jnp.where(core == 0, w_half, theirs), jnp.where(core == 0, theirs, w_half)], axis=1
            )

    for copy in pending:
        copy.wait_send()


def solution(mesh):
    rows, cols = mesh.shape["rows"], mesh.shape["cols"]

    def shards(data_tile, w_factor, h_factor):
        rank, wp = w_factor.shape
        hp = h_factor.shape[1]
        half = data_tile.shape[0] // 2
        wide = pl.cdiv(rank // SUB * wp, LANES) * LANES
        vmem, dma = pltpu.VMEM, pltpu.SemaphoreType.DMA
        return pl.pallas_call(
            functools.partial(kernel, rows, cols),
            out_shape=(
                pltpu.VMEM(w_factor.shape, jnp.float32),
                pltpu.VMEM(h_factor.shape, jnp.float32),
            ),
            in_specs=[pl.BlockSpec(memory_space=pl.ANY)] * 3,
            out_specs=(pl.BlockSpec(memory_space=pltpu.VMEM),) * 2,
            scratch_shapes=[
                vmem(data_tile.shape, jnp.bfloat16),
                vmem(w_factor.shape, jnp.float32),
                vmem(h_factor.shape, jnp.float32),
                vmem((SUB, wide), jnp.float32),
                vmem((cols, SUB, wide), jnp.float32),
                vmem((ITERS, rows, rank, hp), jnp.bfloat16),
                vmem((ITERS, rows, rank + 1, hp), jnp.float32),
                vmem((ITERS, rows, rank + 1, hp), jnp.float32),
                vmem((cols, SUB + 1, wide), jnp.float32),
                vmem((cols, SUB + 1, wide), jnp.float32),
                vmem((ITERS, rank + 1, half), jnp.float32),
                vmem((ITERS, rank + 1, half), jnp.float32),
                vmem((ITERS, cols // 2, rank + 1, half), jnp.float32),
                vmem((ITERS, rank, half), jnp.float32),
                vmem((ITERS, rank, half), jnp.float32),
                dma((3,)),
                dma((cols,)),
                dma((cols,)),
                dma((ITERS, rows)),
                dma((ITERS, rows)),
                dma((ITERS, rows)),
                dma((ITERS, rows)),
                dma((cols,)),
                dma((cols,)),
                dma((ITERS,)),
                dma((ITERS,)),
                dma((ITERS, cols // 2)),
                dma((ITERS, cols // 2)),
                dma((ITERS,)),
                dma((ITERS,)),
            ],
            compiler_params=pltpu.CompilerParams(collective_id=0, has_side_effects=True),
        )(data_tile, w_factor, h_factor)

    placed = (P("rows", "cols"), P(None, ("rows", "cols")), P(None, ("cols", "rows")))
    return jax.shard_map(
        shards,
        mesh=mesh,
        in_specs=placed,
        out_specs=(P(None, ("rows", "cols")), P(None, ("cols", "rows"))),
        check_vma=False,
    )
```

time: 27.3 us -> 24.7 us (0.905)
  Pallas kernels: 24.4 us -> 22.6 us
  local copies, waits for them, and re-layouts: 1.95 us -> 1.22 us
    pallas_call x1, Pallas kernels: 24.4 us -> 22.6 us  [shards(): pl.pallas_call(functools.partial(kernel, rows, cols), out_shape=(pltpu.VM...]
    unnamed x4 -> x2, local copies, waits for them, and re-layouts: 1.95 us -> 1.22 us
where the time goes in v2:
time: 24.7 us; the launch traced here: 24.5 us
  Pallas kernels  22.6 us (91%)
  local copies, waits for them, and re-layouts  1.22 us (5%)
  between operations  0.64 us (3%)
    pallas_call x1, Pallas kernels, shards(): pl.pallas_call(functools.partial(kernel, rows, cols), out_shape=(pltpu.VM...  22.6 us
    unnamed x2, local copies, waits for them, and re-layouts  1.22 us

profile of v2, /device:TPU:0, one launch (start us, length us, event | category | flops | bytes accessed | tf_op | source)
XLA Modules:
  0.0 24.5 jit_solution(7399627548109579537)
XLA Ops:
  0.6 22.6 %shard_map.50 = (f32[32,32]{1,0:T(8,128)S(1)}, f32[32,256]{1,0:T(8,128)S(1)}) custom-call(bf16[256,1024]{1,0:T(8,128)(2,1)} %data_hbm.1, f32[32,32]{1,0:T(8,128)} %w_hbm.1, f32[32,256]{1,0:T(8,128)} %h_hbm.1), custom_call_target="tpu_custom_call" | custom-call | tf_op jit(solution)/shard_map/pallas_call | solution.py:241
  23.3 0.6 %copy.7 = f32[32,32]{1,0:T(8,128)} copy(f32[32,32]{1,0:T(8,128)S(1)} %get-tuple-element.2) | data formatting | bytes 8192
  23.9 0.6 %copy.8 = f32[32,256]{1,0:T(8,128)} copy(f32[32,256]{1,0:T(8,128)S(1)} %get-tuple-element.3) | data formatting | bytes 65536

commit v3 on v2

--- a/solution.py
+++ b/solution.py
@@ -124,10 +124,11 @@
         w_part = jnp.zeros((rank, tr), jnp.float32)
         h_sum = jnp.zeros((SUB, rank), jnp.float32)
         h_sends = []
+        for d in range(1, rows):
+            h_copies[d].wait_recv()
+        kept_chunks = []
         for d in chunk_order(it, rows):
             p = r if d == 0 else r_peers[d - 1][1]
-            if d > 0:
-                h_copies[d].wait_recv()
             h_piece = h_slots[it, d]
             approx = jnp.dot(w_rows, h_piece, preferred_element_type=jnp.float32)
             if hp % LANES == 0:
@@ -140,6 +141,8 @@
                 for k in range(1, per):
                     data = jnp.where(lax.rem(p, per) == k, wide[:, k * hp : (k + 1) * hp], data)
             quotient = (data.astype(jnp.float32) / approx).astype(jnp.bfloat16)
+            kept_chunks.append((d, p, h_piece, quotient))
+        for d, p, h_piece, quotient in kept_chunks:
             h_part = jnp.dot(w_block, quotient, preferred_element_type=jnp.float32)
             h_send[it, d, 0:rank] = h_part
             h_send[it, d, rank : rank + 1, 0:rank] = w_sum
@@ -147,6 +150,8 @@
                 h_sends.append(
                     send(h_send.at[it, d], h_recv.at[it, d], hr_s.at[it, d], hr_r.at[it, d], {"rows": p})
                 )
+
+        for d, p, h_piece, quotient in kept_chunks:
             w_part += lax.dot_general(
                 h_piece, quotient, (((1,), (1,)), ((), ())), preferred_element_type=jnp.float32
             )

time: 24.7 us -> 24.2 us (0.980)
  Pallas kernels: 22.6 us -> 22.1 us
    pallas_call x1, Pallas kernels: 22.6 us -> 22.1 us  [shards(): pl.pallas_call(functools.partial(kernel, rows, cols), out_shape=(pltpu.VM...]
where the time goes in v3:
time: 24.2 us; the launch traced here: 24 us
  Pallas kernels  22.1 us (91%)
  local copies, waits for them, and re-layouts  1.22 us (5%)
  between operations  0.64 us (3%)
    pallas_call x1, Pallas kernels, shards(): pl.pallas_call(functools.partial(kernel, rows, cols), out_shape=(pltpu.VM...  22.1 us
    unnamed x2, local copies, waits for them, and re-layouts  1.22 us

profile of v3, /device:TPU:0, one launch (start us, length us, event | category | flops | bytes accessed | tf_op | source)
XLA Modules:
  0.0 24.0 jit_solution(7478571837866676500)
XLA Ops:
  0.6 22.1 %shard_map.50 = (f32[32,32]{1,0:T(8,128)S(1)}, f32[32,256]{1,0:T(8,128)S(1)}) custom-call(bf16[256,1024]{1,0:T(8,128)(2,1)} %data_hbm.1, f32[32,32]{1,0:T(8,128)} %w_hbm.1, f32[32,256]{1,0:T(8,128)} %h_hbm.1), custom_call_target="tpu_custom_call" | custom-call | tf_op jit(solution)/shard_map/pallas_call | solution.py:246
  22.8 0.6 %copy.7 = f32[32,32]{1,0:T(8,128)} copy(f32[32,32]{1,0:T(8,128)S(1)} %get-tuple-element.2) | data formatting | bytes 8192
  23.4 0.6 %copy.8 = f32[32,256]{1,0:T(8,128)} copy(f32[32,256]{1,0:T(8,128)S(1)} %get-tuple-element.3) | data formatting | bytes 65536

commit v4 on v3

--- a/solution.py
+++ b/solution.py
@@ -64,9 +64,6 @@
     load_w = pltpu.make_async_copy(w_hbm, w_in, local_sem.at[0])
     load_h = pltpu.make_async_copy(h_hbm, h_own, local_sem.at[1])
     load_data = pltpu.make_async_copy(data_hbm, data_v, local_sem.at[2])
-    load_w.start()
-    load_h.start()
-    load_data.start()
 
     c_peers = [(d, partner(c, d, cols)) for d in range(1, cols)]
     r_peers = [(d, partner(r, d, rows)) for d in range(1, rows)]
@@ -77,6 +74,9 @@
     for d, p in reversed(r_peers):
         pl.semaphore_signal(barrier, inc=1, device_id={"rows": p}, device_id_type=MESH)
 
+    load_w.start()
+    load_h.start()
+    load_data.start()
     load_w.wait()
     load_h.wait()
     w_own[:, 0:used] = fold(w_in[...])
@@ -234,6 +234,17 @@
         copy.wait_send()
 
 
+def finish(w_ref, h_ref, w_out, h_out, sems):
+    copies = [
+        pltpu.make_async_copy(w_ref, w_out, sems.at[0]),
+        pltpu.make_async_copy(h_ref, h_out, sems.at[1]),
+    ]
+    for copy in copies:
+        copy.start()
+    for copy in copies:
+        copy.wait()
+
+
 def solution(mesh):
     rows, cols = mesh.shape["rows"], mesh.shape["cols"]
 
@@ -243,7 +254,7 @@
         half = data_tile.shape[0] // 2
         wide = pl.cdiv(rank // SUB * wp, LANES) * LANES
         vmem, dma = pltpu.VMEM, pltpu.SemaphoreType.DMA
-        return pl.pallas_call(
+        w_new, h_new = pl.pallas_call(
             functools.partial(kernel, rows, cols),
             out_shape=(
                 pltpu.VMEM(w_factor.shape, jnp.float32),
@@ -285,6 +296,17 @@
             ],
             compiler_params=pltpu.CompilerParams(collective_id=0, has_side_effects=True),
         )(data_tile, w_factor, h_factor)
+        return pl.pallas_call(
+            finish,
+            out_shape=(
+                jax.ShapeDtypeStruct(w_factor.shape, jnp.float32),
+                jax.ShapeDtypeStruct(h_factor.shape, jnp.float32),
+            ),
+            in_specs=[pl.BlockSpec(memory_space=pltpu.VMEM)] * 2,
+            out_specs=(pl.BlockSpec(memory_space=pl.ANY),) * 2,
+            scratch_shapes=[dma((2,))],
+            compiler_params=pltpu.CompilerParams(vmem_limit_bytes=2**20),
+        )(w_new, h_new)
 
     placed = (P("rows", "cols"), P(None, ("rows", "cols")), P(None, ("cols", "rows")))
     return jax.shard_map(

time: 24.2 us -> 23.6 us (0.975)
  local copies, waits for them, and re-layouts: 1.22 us -> 0 us
  Pallas kernels: 22.1 us -> 22.8 us
    unnamed x2 -> x0, local copies, waits for them, and re-layouts: 1.22 us -> none
    pallas_call x0 -> x1, Pallas kernels: none -> 0.64 us  [shards(): pl.pallas_call(finish, out_shape=(jax.ShapeDtypeStruct(w_factor.shape, jn...]
where the time goes in v4:
time: 23.6 us; the launch traced here: 23.4 us
  Pallas kernels  22.8 us (97%)
  between operations  0.64 us (3%)
    pallas_call x1, Pallas kernels, shards(): pl.pallas_call(functools.partial(kernel, rows, cols), out_shape=(pltpu.VM...  22.1 us
    pallas_call x1, Pallas kernels, shards(): pl.pallas_call(finish, out_shape=(jax.ShapeDtypeStruct(w_factor.shape, jn...  0.64 us

profile of v4, /device:TPU:0, one launch (start us, length us, event | category | flops | bytes accessed | tf_op | source)
XLA Modules:
  0.0 23.4 jit_solution(9993865087104731990)
XLA Ops:
  0.6 22.1 %shard_map.50 = (f32[32,32]{1,0:T(8,128)S(1)}, f32[32,256]{1,0:T(8,128)S(1)}) custom-call(bf16[256,1024]{1,0:T(8,128)(2,1)} %data_hbm.1, f32[32,32]{1,0:T(8,128)} %w_hbm.1, f32[32,256]{1,0:T(8,128)} %h_hbm.1), custom_call_target="tpu_custom_call" | custom-call | tf_op jit(solution)/shard_map/pallas_call | solution.py:257
  22.8 0.6 %shard_map.51 = (f32[32,32]{1,0:T(8,128)}, f32[32,256]{1,0:T(8,128)}) custom-call(f32[32,32]{1,0:T(8,128)S(1)} %get-tuple-element.4.w_ref, f32[32,256]{1,0:T(8,128)S(1)} %get-tuple-element.5.h_ref), custom_call_target="tpu_custom_call" | custom-call | tf_op jit(solution)/shard_map/pallas_call | solution.py:299

commit v5 on v4

--- a/solution.py
+++ b/solution.py
@@ -203,10 +203,9 @@
             w_now = w_f32[:, 0:wp]
             for p in range(1, cols):
                 w_now = jnp.where(c == p, w_f32[:, p * wp : (p + 1) * wp], w_now)
-            for copy in w_sends:
+            numer, total = w_send[c, 0:SUB, 0:used], w_send[c, SUB : SUB + 1, 0:rank]
+            for (d, p), copy in zip(c_peers, reversed(w_sends)):
                 copy.wait_recv()
-            numer, total = w_send[c, 0:SUB, 0:used], w_send[c, SUB : SUB + 1, 0:rank]
-            for d, p in c_peers:
                 numer += w_recv[d, 0:SUB, 0:used]
                 total += w_recv[d, SUB : SUB + 1, 0:rank]
             numer = unfold(numer, groups, wp)

time: 23.6 us -> 23.6 us (level)
  no operation moved by 1% of the time
where the time goes in v5:
time: 23.6 us; the launch traced here: 23.4 us
  Pallas kernels  22.7 us (96%)
  between operations  0.64 us (3%)
    pallas_call x1, Pallas kernels, shards(): pl.pallas_call(functools.partial(kernel, rows, cols), out_shape=(pltpu.VM...  22.1 us
    pallas_call x1, Pallas kernels, shards(): pl.pallas_call(finish, out_shape=(jax.ShapeDtypeStruct(w_factor.shape, jn...  0.64 us

profile of v5, /device:TPU:0, one launch (start us, length us, event | category | flops | bytes accessed | tf_op | source)
XLA Modules:
  0.0 23.4 jit_solution(3519412858709168026)
XLA Ops:
  0.6 22.1 %shard_map.50 = (f32[32,32]{1,0:T(8,128)S(1)}, f32[32,256]{1,0:T(8,128)S(1)}) custom-call(bf16[256,1024]{1,0:T(8,128)(2,1)} %data_hbm.1, f32[32,32]{1,0:T(8,128)} %w_hbm.1, f32[32,256]{1,0:T(8,128)} %h_hbm.1), custom_call_target="tpu_custom_call" | custom-call | tf_op jit(solution)/shard_map/pallas_call | solution.py:256
  22.7 0.6 %shard_map.51 = (f32[32,32]{1,0:T(8,128)}, f32[32,256]{1,0:T(8,128)}) custom-call(f32[32,32]{1,0:T(8,128)S(1)} %get-tuple-element.4.w_ref, f32[32,256]{1,0:T(8,128)S(1)} %get-tuple-element.5.h_ref), custom_call_target="tpu_custom_call" | custom-call | tf_op jit(solution)/shard_map/pallas_call | solution.py:298
